TPU v7x, 32 devices: a whole 2x2x4 slice. The times are simulated.
32 devices in a mesh: row: 8 (over z, core), col: 4 (over y, x).
Axes of the slice: x: 2, y: 2, z: 4, core: 2. Of those that a mesh axis runs over, the one named last changes fastest.
Arguments:
- shot_traces: float32 [16384, 2, 8192], P(('row', 'col')), may hold values from -0.046875 to 0.046875
- shot_ids: int32 [16384], P(('row', 'col')), may hold values from 0 to 8191, as said below
- shot_counts: int32 [32], P(('row', 'col')), may hold values from 0 to 512, as said below
- missing_blocks: int32 [64, 64], P('row', 'col'), may hold values from 0 to 1, as said below
- weight_bins: int32 [8192], P(('row', 'col')), may hold values from 0 to 63
- weight_table: float32 [64], replicated, may hold values from 0.1 to 1
- focus_panel: float32 [2, 8192, 512], P(None, ('col', 'row')), may hold values from -6 to 6
Outputs:
- wavefield: float32 [2, 8192, 512], P(None, ('row', 'col'))
- adjoint_image: float32 [2, 8192, 512], P(None, ('col', 'row'))
Inputs may be any that keep to these rules, and one draw needn't show every extreme that they name: `shot_ids`: over the counted slots of all devices every source appears exactly once; uncounted slots hold arbitrary sources. The counted slots of one device hold at most 64 sources of any block of 1024 consecutive sources, and at most (128) of any block of 2048; some device reaches both. `shot_counts`: some device has all 512 slots counted. `missing_blocks`: diagonal blocks are recorded, and of two mirrored blocks at most one is missing.
All inputs are finite; a program needn't handle non-finite values.
Results may differ from a plain program's by a relative error of at most 0.00007.
Values sent between devices are 32-bit elements; how exact they have to be, the bound alone decides.
A program may use at most 320 MiB of HBM per device.

v0:
```python
import jax
import jax.numpy as jnp
from jax import lax
from jax.sharding import PartitionSpec as P


def high_dot(left, right):
    return jnp.dot(left, right, precision=lax.Precision.HIGHEST, preferred_element_type=jnp.float32)


def trans_dot(left, right):
    return lax.dot_general(
        left,
        right,
        (((0,), (0,)), ((), ())),
        precision=lax.Precision.HIGHEST,
        preferred_element_type=jnp.float32,
    )


def pack_slots(traces, labels, held_count, group_size, group_count, capacity):
    slot_total = labels.shape[0]
    slot_index = jnp.arange(slot_total, dtype=jnp.int32)
    is_used = slot_index < held_count
    dest_group = labels // group_size
    onehot = (
        (dest_group[:, None] == jnp.arange(group_count, dtype=jnp.int32)[None, :])
        & is_used[:, None]
    ).astype(jnp.int32)
    before = jnp.cumsum(onehot, axis=0) - onehot
    rank_in = jnp.sum(before * onehot, axis=1)
    position = jnp.where(is_used, dest_group * capacity + rank_in, group_count * capacity)
    source = (
        jnp.full((group_count * capacity,), slot_total, jnp.int32)
        .at[position]
        .set(slot_index, mode="drop")
    )
    packed = jnp.take(traces, source, axis=0, mode="fill", fill_value=0.0)
    packed_labels = jnp.take(labels, source, axis=0, mode="fill", fill_value=-1)
    return (packed, packed_labels)


def place_rows(arrived, labels, first_label, length):
    has_label = labels >= 0
    target = jnp.where(has_label, labels - first_label, length)
    source = (
        jnp.zeros((length,), jnp.int32)
        .at[target]
        .set(jnp.arange(labels.shape[0], dtype=jnp.int32), mode="drop")
    )
    return jnp.take(arrived, source, axis=0)


def lookup(bins, table):
    matches = bins[:, None] == jnp.arange(table.shape[0], dtype=jnp.int32)[None, :]
    return jnp.sum(jnp.where(matches, table[None, :], 0.0), axis=1)


def local(
    shot_traces, shot_ids, shot_counts, missing_blocks, weight_bins, weight_table, focus_panel
):
    slot_total = shot_traces.shape[0]
    stations = shot_traces.shape[2]
    row_count = lax.axis_size("row")
    col_count = lax.axis_size("col")
    src_tile = stations // row_count
    rcv_tile = stations // col_count
    row_index = lax.axis_index("row")
    col_index = lax.axis_index("col")
    held_count = shot_counts[0]
    packed, packed_labels = pack_slots(
        shot_traces, shot_ids, held_count, src_tile, row_count, slot_total // row_count
    )
    outgoing = packed.reshape(slot_total, 2, col_count, rcv_tile)
    label_copies = jnp.broadcast_to(packed_labels[:, None, None], (slot_total, 1, col_count))
    arrived, arrived_labels = (
        lax.all_to_all(
            lax.all_to_all(outgoing, "row", split_axis=0, concat_axis=0, tiled=True),
            "col",
            split_axis=2,
            concat_axis=0,
            tiled=True,
        ),
        lax.all_to_all(
            lax.all_to_all(label_copies, "row", split_axis=0, concat_axis=0, tiled=True),
            "col",
            split_axis=2,
            concat_axis=0,
            tiled=True,
        ),
    )
    direct = place_rows(
        arrived.reshape(-1, 2, rcv_tile), arrived_labels.reshape(-1), row_index * src_tile, src_tile
    )
    capacity_rec = slot_total // col_count
    packed_mirror, mirror_labels = pack_slots(
        shot_traces, shot_ids, held_count, rcv_tile, col_count, capacity_rec
    )
    mirror_out = packed_mirror.reshape(slot_total, 2, row_count, src_tile)
    mirror_copies = jnp.broadcast_to(mirror_labels[:, None, None], (slot_total, 1, row_count))
    halfway, halfway_labels = (
        lax.all_to_all(mirror_out, "row", split_axis=2, concat_axis=0, tiled=True),
        lax.all_to_all(mirror_copies, "row", split_axis=2, concat_axis=0, tiled=True),
    )
    halfway = halfway.reshape(row_count, col_count, capacity_rec, 2, src_tile)
    halfway_labels = halfway_labels.reshape(row_count, col_count, capacity_rec)
    mirrored, mirrored_labels = (
        lax.all_to_all(halfway, "col", split_axis=1, concat_axis=0, tiled=True),
        lax.all_to_all(halfway_labels, "col", split_axis=1, concat_axis=0, tiled=True),
    )
    transposed = place_rows(
        mirrored.reshape(-1, 2, src_tile),
        mirrored_labels.reshape(-1),
        col_index * rcv_tile,
        rcv_tile,
    )
    blocks_down = missing_blocks.shape[0]
    blocks_across = missing_blocks.shape[1]
    block_size = src_tile // blocks_down
    is_missing = jnp.broadcast_to(
        missing_blocks[:, None, :, None] > 0, (blocks_down, block_size, blocks_across, block_size)
    ).reshape(src_tile, rcv_tile)
    kernel_re = jnp.where(is_missing, transposed[:, 0, :].T, direct[:, 0, :])
    kernel_im = jnp.where(is_missing, transposed[:, 1, :].T, direct[:, 1, :])
    focus_all = lax.all_gather(focus_panel, "row", axis=1, tiled=True)
    panel_re = focus_all[0]
    panel_im = focus_all[1]
    field_re = high_dot(kernel_re, panel_re) - high_dot(kernel_im, panel_im)
    field_im = high_dot(kernel_re, panel_im) + high_dot(kernel_im, panel_re)
    own_rows = lax.psum_scatter(
        jnp.stack([field_re, field_im], axis=1), "col", scatter_dimension=0, tiled=True
    )
    weighted = own_rows * lookup(weight_bins, weight_table)[:, None, None]
    weighted_all = lax.all_gather(weighted, "col", axis=0, tiled=True)
    weighted_re = weighted_all[:, 0, :]
    weighted_im = weighted_all[:, 1, :]
    image_re = trans_dot(kernel_re, weighted_re) + trans_dot(kernel_im, weighted_im)
    image_im = trans_dot(kernel_re, weighted_im) - trans_dot(kernel_im, weighted_re)
    image_rows = lax.psum_scatter(
        jnp.stack([image_re, image_im], axis=1), "row", scatter_dimension=0, tiled=True
    )
    return (jnp.swapaxes(own_rows, 0, 1), jnp.swapaxes(image_rows, 0, 1))


def solution(mesh):
    placed = (
        P(("row", "col"), None, None),
        P(("row", "col")),
        P(("row", "col")),
        P("row", "col"),
        P(("row", "col")),
        P(),
        P(None, ("col", "row"), None),
    )
    return jax.shard_map(
        local,
        mesh=mesh,
        in_specs=placed,
        out_specs=(P(None, ("row", "col"), None), P(None, ("col", "row"), None)),
        check_vma=False,
    )
```

profile of v0, /device:TPU:0, one launch (start us, length us, event | category | flops | bytes accessed | tf_op | source)
XLA Modules:
  0.0 3004.8 jit_solution(7320027503806781261)
XLA Ops:
  49.6 45.2 %gather_fusion.3 = f32[512,2,8192]{2,1,0:T(2,128)} fusion(f32[512,2,8192]{2,1,0:T(2,128)} %param.11, s32[1024]{0:T(1024)S(1)} %pad_clamp_fusion.1), kind=kCustom, calls=%fused_computation.1.clone | custom fusion | bytes 67110912 | tf_op jit(solution)/shard_map/jit(_take)/gather | solution.py:38
  100.2 24.2 broadcast_select_fusion.1
  124.4 48.8 %copy.56 = f32[512,2,8192]{0,2,1:T(8,128)} copy(f32[512,2,8192]{2,1,0:T(2,128)} %broadcast_select_fusion.1) | data formatting | bytes 67108864 | tf_op jit(solution)/shard_map/jit(_take)/select_n | solution.py:38
  173.1 22.9 copy.57
  203.9 46.5 %gather_fusion.5 = f32[512,2,8192]{2,1,0:T(2,128)} fusion(f32[512,2,8192]{2,1,0:T(2,128)} %param.11, s32[1024]{0:T(1024)S(1)} %pad_clamp_fusion), kind=kCustom, calls=%fused_computation.3.clone | custom fusion | bytes 67110912 | tf_op jit(solution)/shard_map/jit(_take)/gather | solution.py:38
  250.5 24.2 broadcast_select_fusion
  274.6 48.7 %copy.64 = f32[512,2,8192]{0,2,1:T(8,128)} copy(f32[512,2,8192]{2,1,0:T(2,128)} %broadcast_select_fusion) | data formatting | bytes 67108864 | tf_op jit(solution)/shard_map/jit(_take)/select_n | solution.py:38
  323.4 39.8 %copy.65 = f32[512,2,4,2048]{3,2,1,0:T(4,128)} copy(f32[512,2,4,2048]{0,3,2,1:T(8,128)} %bitcast.133) | data formatting | bytes 67108864 | tf_op jit(solution)/shard_map/reshape | solution.py:74
  363.2 563.9 %all-to-all-done.2 = f32[512,2,8,1024]{0,3,1,2:T(8,128)} async-done(((f32[512,2,8,1024]{0,3,1,2:T(8,128)}), f32[512,2,8,1024]{0,3,1,2:T(8,128)}, u32[]{:S(2)}, u32[]{:S(2)}) %all-to-all-start.2) | async-done | bytes 33554464 | tf_op jit(solution)/shard_map/all_to_all | solution.py:102
  934.2 31.9 %copy.58 = f32[512,2,8,1024]{3,0,1,2:T(8,128)} copy(f32[512,2,8,1024]{0,3,1,2:T(8,128)} %all-to-all-done.2) | data formatting | bytes 67108864 | tf_op jit(solution)/shard_map/all_to_all | solution.py:102
  966.1 23.4 copy.59
  989.5 667.9 %all-to-all-done.6 = f32[512,2,4,2048]{3,2,1,0:T(4,128)} async-done(((f32[512,2,4,2048]{3,2,1,0:T(4,128)}), f32[512,2,4,2048]{3,2,1,0:T(4,128)}, u32[]{:S(2)}, u32[]{:S(2)}) %all-to-all-start.6) | async-done | bytes 33554464 | tf_op jit(solution)/shard_map/all_to_all | solution.py:78
  1667.1 37.9 %copy.66 = f32[512,2,4,2048]{0,3,1,2:T(8,128)} copy(f32[512,2,4,2048]{3,2,1,0:T(4,128)} %all-to-all-done.6) | data formatting | bytes 67108864 | tf_op jit(solution)/shard_map/all_to_all | solution.py:78
  1705.0 324.4 %all-to-all-done.3 = f32[8,4,128,2,1024]{4,2,3,0,1:T(8,128)} async-done(((f32[8,4,128,2,1024]{4,2,3,0,1:T(8,128)}), f32[8,4,128,2,1024]{4,2,3,0,1:T(8,128)}, u32[]{:S(2)}, u32[]{:S(2)}) %all-to-all-start.3) | async-done | bytes 33554464 | tf_op jit(solution)/shard_map/all_to_all | solution.py:108
  2048.2 15.9 scatter_custom_fusion.1
  2064.1 23.5 copy.60
  2087.6 55.0 %copy.61 = f32[4096,2,1024]{2,1,0:T(2,128)} copy(f32[4096,2,1024]{2,0,1:T(8,128)} %bitcast.135) | data formatting | bytes 67108864 | tf_op jit(solution)/shard_map/reshape | solution.py:112
  2142.7 258.0 %all-to-all-done.7 = f32[512,2,4,2048]{0,3,1,2:T(8,128)} async-done(((f32[512,2,4,2048]{0,3,1,2:T(8,128)}), f32[512,2,4,2048]{0,3,1,2:T(8,128)}, u32[]{:S(2)}, u32[]{:S(2)}) %all-to-all-start.7) | async-done | bytes 33554464 | tf_op jit(solution)/shard_map/all_to_all | solution.py:77
  2400.6 31.8 %copy.67 = f32[512,2,4,2048]{3,0,2,1:T(8,128)} copy(f32[512,2,4,2048]{0,3,1,2:T(8,128)} %all-to-all-done.7) | data formatting | bytes 67108864 | tf_op jit(solution)/shard_map/all_to_all | solution.py:77
  2432.4 55.0 %copy.68 = f32[2048,2,2048]{2,1,0:T(2,128)} copy(f32[2048,2,2048]{2,0,1:T(8,128)} %bitcast.136) | data formatting | bytes 67108864 | tf_op jit(solution)/shard_map/reshape | solution.py:93
  2487.5 39.4 %gather_fusion.1 = f32[1024,2,2048]{2,1,0:T(2,128)} fusion(f32[2048,2,2048]{2,1,0:T(2,128)} %copy.68, s32[1024]{0:T(1024)S(1)} %fusion.22), kind=kCustom, calls=%fused_computation.5 | custom fusion | bytes 33558528 | tf_op jit(solution)/shard_map/jit(_take)/gather | solution.py:51
  2526.9 25.0 copy.69
  2551.9 54.2 %gather_fusion = f32[2048,2,1024]{2,1,0:T(2,128)} fusion(f32[4096,2,1024]{2,1,0:T(2,128)} %copy.61, s32[2048]{0:T(1024)S(1)} %fusion.19), kind=kCustom, calls=%fused_computation.4 | custom fusion | bytes 33562624 | tf_op jit(solution)/shard_map/jit(_take)/gather | solution.py:51
  2635.7 19.2 fusion.31
  2655.6 17.8 fusion.1
  2673.4 16.7 fusion.3
  2733.9 51.4 %reduce-scatter.3.cloned.1.call-done = f32[256,2,512]{2,0,1:T(8,128)} async-done(((f32[1024,2,512]{2,0,1:T(8,128)}), f32[256,2,512]{2,0,1:T(8,128)}) %reduce-scatter.3.cloned.1.call-update) | async-done | bytes 1048592 | tf_op jit(solution)/shard_map/reduce_scatter | solution.py:130
  2787.7 52.7 %all-gather.5.cloned.1.call-done = f32[1024,2,512]{2,0,1:T(8,128)} async-done(((f32[256,2,512]{2,0,1:T(8,128)}), f32[1024,2,512]{2,0,1:T(8,128)}) %all-gather.5.cloned.1.call-update) | async-done | bytes 4194320 | tf_op jit(solution)/shard_map/all_gather | solution.py:134
  2840.4 17.2 fusion.6
  2857.7 16.0 fusion.7
  2888.8 15.1 subtract_bitcast_fusion
  2908.2 89.7 %reduce-scatter.5.cloned.1.call-done = f32[256,2,512]{2,0,1:T(8,128)} async-done(((f32[2048,2,512]{2,0,1:T(8,128)}), f32[256,2,512]{2,0,1:T(8,128)}) %reduce-scatter.5.cloned.1.call-update) | async-done | bytes 1048592 | tf_op jit(solution)/shard_map/reduce_scatter | solution.py:139
  (114 shorter events, 186.1 us)
Async XLA Ops:
  22.1 12.5 all-to-all-start.4
  35.1 10.7 all-to-all-start
  45.9 49.6 %all-to-all-start.5 = ((s32[512,1,4]{0,1,2:T(1,128)}), s32[512,1,4]{0,1,2:T(1,128)S(1)}, u32[]{:S(2)}, u32[]{:S(2)}) async-start(s32[512,1,4]{0,1,2:T(1,128)} %copy.63), calls=%async_computation.5 | async-start | bytes 16384 | tf_op jit(solution)/shard_map/all_to_all | solution.py:84
  95.5 0.6 copy-start.5
  96.1 100.0 %all-to-all-start.1 = ((s32[8,4,128]{2,0,1:T(8,128)}), s32[8,4,128]{2,0,1:T(8,128)S(1)}, u32[]{:S(2)}, u32[]{:S(2)}) async-start(s32[8,4,128]{2,0,1:T(8,128)} %bitcast.127), calls=%async_computation.1 | async-start | bytes 32768 | tf_op jit(solution)/shard_map/all_to_all | solution.py:109
  196.0 0.6 copy-start.3
  196.6 730.5 %all-to-all-start.2 = ((f32[512,2,8,1024]{0,3,1,2:T(8,128)}), f32[512,2,8,1024]{0,3,1,2:T(8,128)}, u32[]{:S(2)}, u32[]{:S(2)}) async-start(f32[512,2,8,1024]{0,3,1,2:T(8,128)} %copy.57), calls=%async_computation.2 | async-start | bytes 67108864 | tf_op jit(solution)/shard_map/all_to_all | solution.py:102
  927.1 730.3 %all-to-all-start.6 = ((f32[512,2,4,2048]{3,2,1,0:T(4,128)}), f32[512,2,4,2048]{3,2,1,0:T(4,128)}, u32[]{:S(2)}, u32[]{:S(2)}) async-start(f32[512,2,4,2048]{3,2,1,0:T(4,128)} %copy.65), calls=%async_computation.6 | async-start | bytes 67108864 | tf_op jit(solution)/shard_map/all_to_all | solution.py:78
  1657.4 372.0 %all-to-all-start.3 = ((f32[8,4,128,2,1024]{4,2,3,0,1:T(8,128)}), f32[8,4,128,2,1024]{4,2,3,0,1:T(8,128)}, u32[]{:S(2)}, u32[]{:S(2)}) async-start(f32[8,4,128,2,1024]{4,2,3,0,1:T(8,128)} %copy.59), calls=%async_computation.3 | async-start | bytes 67108864 | tf_op jit(solution)/shard_map/all_to_all | solution.py:108
  1705.0 334.9 %copy-start.7 = (s32[8,16]{1,0:T(8,128)S(1)}, s32[8,16]{1,0:T(8,128)}, u32[]{:S(2)}) copy-start(s32[8,16]{1,0:T(8,128)} %param.14) | copy-start | bytes 1540
  1705.0 335.0 %copy-start.6 = (s32[512,1,4]{0,1,2:T(1,128)S(1)}, s32[512,1,4]{0,1,2:T(1,128)}, u32[]{:S(2)}) copy-start(s32[512,1,4]{0,1,2:T(1,128)} %copy-done.5) | copy-start | bytes 24580
  1705.0 343.1 %copy-start.4 = (s32[8,4,128]{2,0,1:T(8,128)S(1)}, s32[8,4,128]{2,0,1:T(8,128)}, u32[]{:S(2)}) copy-start(s32[8,4,128]{2,0,1:T(8,128)} %copy-done.3) | copy-start | bytes 49156
  2029.4 371.3 %all-to-all-start.7 = ((f32[512,2,4,2048]{0,3,1,2:T(8,128)}), f32[512,2,4,2048]{0,3,1,2:T(8,128)}, u32[]{:S(2)}, u32[]{:S(2)}) async-start(f32[512,2,4,2048]{0,3,1,2:T(8,128)} %copy.66), calls=%async_computation.7 | async-start | bytes 67108864 | tf_op jit(solution)/shard_map/all_to_all | solution.py:77
  2039.1 634.3 %all-gather.3.cloned.1.call-start = ((), (), s32[]{:S(2)}) async-start(), calls=%async_computation.10 | async-start | bytes 9437184 | tf_op jit(solution)/shard_map/all_gather | solution.py:125
  2039.8 745.5 %reduce-scatter.3.cloned.1.call-start = ((), (), s32[]{:S(2)}) async-start(), calls=%async_computation.11 | async-start | bytes 5242880 | tf_op jit(solution)/shard_map/reduce_scatter | solution.py:130
  2606.1 16.5 copy-start.1
  2673.4 16.8 copy-start
  2673.4 16.8 copy-start.10
  2690.2 27.4 slice-start.2
  2703.9 13.6 slice-start.3
  2731.3 2.5 copy-start.8
  2731.3 2.5 copy-start.9
  2733.8 106.6 %all-gather.5.cloned.1.call-start = ((), (), s32[]{:S(2)}) async-start(), calls=%async_computation.12 | async-start | bytes 5242880 | tf_op jit(solution)/shard_map/all_gather | solution.py:134
  2787.7 210.2 %reduce-scatter.5.cloned.1.call-start = ((), (), s32[]{:S(2)}) async-start(), calls=%async_computation.13 | async-start | bytes 9437184 | tf_op jit(solution)/shard_map/reduce_scatter | solution.py:139
  2840.4 17.3 copy-start.2
  2840.4 33.3 %slice-start = ((s8[8388608]{0:T(1024)(128)(4,1)}), s8[4194304]{0:T(1024)(128)(4,1)S(1)}, s32[]{:S(2)}) async-start(s8[8388608]{0:T(1024)(128)(4,1)} %bitcast.137), calls=%async_computation.14 | async-start | bytes 8388608
  2857.7 16.0 slice-start.1
Sparse Core Ops, SparseCore 0:
  2041.5 81.8 all-gather.2
  2733.9 51.3 reduce-scatter.2
  2787.8 52.5 all-gather.4
  2908.3 89.5 reduce-scatter.4
where the time goes:
time: 3020 us; the launch traced here: 3000 us
  waiting for transfers between devices  2010 us (67%)
  local copies, waits for them, and re-layouts  696 us (23%)
  matrix products  121 us (4%)
  other arithmetic  106 us (4%)
  starting transfers between devices  53.3 us (2%)
    all_to_all x1, waiting for transfers between devices, local(): lax.all_to_all(outgoing, 'row', split_axis=0, concat_axis=0, tiled=True)  668 us
    all_to_all x1, waiting for transfers between devices, local(): lax.all_to_all(mirror_out, 'row', split_axis=2, concat_axis=0, tiled=True)  564 us
    all_to_all x1, waiting for transfers between devices, local(): lax.all_to_all(halfway, 'col', split_axis=1, concat_axis=0, tiled=True)  324 us
    all_to_all x1, waiting for transfers between devices, local(): lax.all_to_all(lax.all_to_all(outgoing, 'row', split_axis=0, concat_axis=...  258 us
    gather x3, local copies, waits for them, and re-layouts, place_rows(): return jnp.take(arrived, source, axis=0)  119 us
    select_n x2, local copies, waits for them, and re-layouts, pack_slots(): packed = jnp.take(traces, source, axis=0, mode='fill', fill_value=0.0)  97.5 us
    gather x2, local copies, waits for them, and re-layouts, pack_slots(): packed = jnp.take(traces, source, axis=0, mode='fill', fill_value=0.0)  91.8 us
    reduce_scatter x1, waiting for transfers between devices, local(): lax.psum_scatter(jnp.stack([image_re, image_im], axis=1), 'row', scatter_...  89.7 us
  transfers between devices with their start and end apart: 12, of which 8 were waited for; matrix products, arithmetic and copies ran while one was open for 26% of the time, Pallas kernels for 0%

commit v1 on v0

--- a/solution.py
+++ b/solution.py
@@ -74,12 +74,20 @@
     outgoing = packed.reshape(slot_total, 2, col_count, rcv_tile)
     label_copies = jnp.broadcast_to(packed_labels[:, None, None], (slot_total, 1, col_count))
     arrived, arrived_labels = (
-        lax.all_to_all(
-            lax.all_to_all(outgoing, "row", split_axis=0, concat_axis=0, tiled=True),
-            "col",
-            split_axis=2,
-            concat_axis=0,
-            tiled=True,
+        jnp.concatenate(
+            lax.all_to_all(
+                jnp.stack(
+                    jnp.split(
+                        lax.all_to_all(outgoing, "row", split_axis=0, concat_axis=0, tiled=True),
+                        lax.axis_size("col"),
+                        axis=2,
+                    )
+                ),
+                "col",
+                0,
+                0,
+            ),
+            axis=0,
         ),
         lax.all_to_all(
             lax.all_to_all(label_copies, "row", split_axis=0, concat_axis=0, tiled=True),

time: 3020 us -> 2930 us (0.970)
  local copies, waits for them, and re-layouts: 696 us -> 506 us
  waiting for transfers between devices: 2010 us -> 2100 us
    reshape x2 -> x0, local copies, waits for them, and re-layouts: 94.8 us -> none  [the longest x1 55 us: local(): arrived.reshape(-1, 2, rcv_tile)]
    all_to_all x1, waiting for transfers between devices: 564 us -> 652 us  [local(): lax.all_to_all(mirror_out, 'row', split_axis=2, concat_axis=0, tiled=True)]
    all_to_all x2 -> x0, local copies, waits for them, and re-layouts: 69.7 us -> none  [the longest x1 37.9 us: local(): lax.all_to_all(outgoing, 'row', split_axis=0, concat_axis=0, tiled=True)]
    select_n x2 -> x1, local copies, waits for them, and re-layouts: 97.5 us -> 48.7 us  [pack_slots(): packed = jnp.take(traces, source, axis=0, mode='fill', fill_value=0.0)]
  transfers between devices with their start and end apart: 12 -> 12, of which waited for: 8 -> 8; matrix products, arithmetic and copies ran while one was open for 26% -> 21% of each run, Pallas kernels for 0% -> 0%
where the time goes in v1:
time: 2930 us; the launch traced here: 2920 us
  waiting for transfers between devices  2100 us (72%)
  local copies, waits for them, and re-layouts  506 us (17%)
  other arithmetic  127 us (4%)
  matrix products  121 us (4%)
  starting transfers between devices  53.4 us (2%)
    all_to_all x1, waiting for transfers between devices, local(): lax.all_to_all(outgoing, 'row', split_axis=0, concat_axis=0, tiled=True)  668 us
    all_to_all x1, waiting for transfers between devices, local(): lax.all_to_all(mirror_out, 'row', split_axis=2, concat_axis=0, tiled=True)  652 us
    all_to_all x1, waiting for transfers between devices, local(): lax.all_to_all(halfway, 'col', split_axis=1, concat_axis=0, tiled=True)  319 us
    all_to_all x1, waiting for transfers between devices, local(): lax.all_to_all(jnp.stack(jnp.split(lax.all_to_all(outgoing, 'row', split_...  258 us
    gather x3, local copies, waits for them, and re-layouts, place_rows(): return jnp.take(arrived, source, axis=0)  119 us
    gather x2, local copies, waits for them, and re-layouts, pack_slots(): packed = jnp.take(traces, source, axis=0, mode='fill', fill_value=0.0)  91.8 us
    reduce_scatter x1, waiting for transfers between devices, local(): lax.psum_scatter(jnp.stack([image_re, image_im], axis=1), 'row', scatter_...  89.7 us
    dot_general x4, matrix products, trans_dot(): lax.dot_general(left, right, (((0,), (0,)), ((), ())), precision=lax.Prec...  63.5 us
  transfers between devices with their start and end apart: 12, of which 8 were waited for; matrix products, arithmetic and copies ran while one was open for 21% of the time, Pallas kernels for 0%

profile of v1, /device:TPU:0, one launch (start us, length us, event | category | flops | bytes accessed | tf_op | source)
XLA Modules:
  0.0 2918.0 jit_solution(6057759850904522265)
XLA Ops:
  49.6 45.2 %gather_fusion.3 = f32[512,2,8192]{2,1,0:T(2,128)} fusion(f32[512,2,8192]{2,1,0:T(2,128)} %param.11, s32[1024]{0:T(1024)S(1)} %pad_clamp_fusion.1), kind=kCustom, calls=%fused_computation.1.clone | custom fusion | bytes 67110912 | tf_op jit(solution)/shard_map/jit(_take)/gather | solution.py:38
  100.2 24.2 broadcast_select_fusion.1
  124.4 48.7 %copy.57 = f32[512,2,8192]{0,2,1:T(8,128)} copy(f32[512,2,8192]{2,1,0:T(2,128)} %broadcast_select_fusion.1) | data formatting | bytes 67108864 | tf_op jit(solution)/shard_map/jit(_take)/select_n | solution.py:38
  173.1 22.9 copy.58
  203.9 46.5 %gather_fusion.5 = f32[512,2,8192]{2,1,0:T(2,128)} fusion(f32[512,2,8192]{2,1,0:T(2,128)} %param.11, s32[1024]{0:T(1024)S(1)} %pad_clamp_fusion), kind=kCustom, calls=%fused_computation.3.clone | custom fusion | bytes 67110912 | tf_op jit(solution)/shard_map/jit(_take)/gather | solution.py:38
  250.4 24.2 broadcast_select_fusion
  274.6 652.4 %all-to-all-done.2 = f32[512,2,8,1024]{0,3,1,2:T(8,128)} async-done(((f32[512,2,8,1024]{0,3,1,2:T(8,128)}), f32[512,2,8,1024]{0,3,1,2:T(8,128)}, u32[]{:S(2)}, u32[]{:S(2)}) %all-to-all-start.2) | async-done | bytes 33554464 | tf_op jit(solution)/shard_map/all_to_all | solution.py:110
  934.2 31.8 %copy.59 = f32[512,2,8,1024]{3,0,1,2:T(8,128)} copy(f32[512,2,8,1024]{0,3,1,2:T(8,128)} %all-to-all-done.2) | data formatting | bytes 67108864 | tf_op jit(solution)/shard_map/all_to_all | solution.py:110
  966.1 23.4 copy.60
  989.5 667.9 %all-to-all-done.6 = f32[512,2,4,2048]{3,1,2,0:T(2,128)} async-done(((f32[512,2,4,2048]{3,1,2,0:T(2,128)}), f32[512,2,4,2048]{3,1,2,0:T(2,128)}, u32[]{:S(2)}, u32[]{:S(2)}) %all-to-all-start.6) | async-done | bytes 33554464 | tf_op jit(solution)/shard_map/all_to_all | solution.py:81
  1667.1 22.8 slice_bitcast_fusion.5
  1689.9 20.1 pad_maximum_fusion
  1710.0 319.3 %all-to-all-done.3 = f32[8,4,128,2,1024]{4,2,3,0,1:T(8,128)} async-done(((f32[8,4,128,2,1024]{4,2,3,0,1:T(8,128)}), f32[8,4,128,2,1024]{4,2,3,0,1:T(8,128)}, u32[]{:S(2)}, u32[]{:S(2)}) %all-to-all-start.3) | async-done | bytes 33554464 | tf_op jit(solution)/shard_map/all_to_all | solution.py:116
  2048.2 15.9 scatter_custom_fusion.1
  2064.1 23.5 copy.61
  2087.6 55.0 %copy.62 = f32[4096,2,1024]{2,1,0:T(2,128)} copy(f32[4096,2,1024]{2,0,1:T(8,128)} %bitcast.145) | data formatting | bytes 67108864 | tf_op jit(solution)/shard_map/reshape | solution.py:120
  2142.7 258.0 %all-to-all-done.7 = f32[4,512,2,1,2048]{4,2,1,3,0:T(2,128)} async-done(((f32[4,512,2,1,2048]{4,2,1,3,0:T(2,128)}), f32[4,512,2,1,2048]{4,2,1,3,0:T(2,128)}, u32[]{:S(2)}, u32[]{:S(2)}) %all-to-all-start.7) | async-done | bytes 33554464 | tf_op jit(solution)/shard_map/all_to_all | solution.py:78
  2400.7 39.4 %gather_fusion.1 = f32[1024,2,2048]{2,1,0:T(2,128)} fusion(f32[2048,2,2048]{2,1,0:T(2,128)} %bitcast.34, s32[1024]{0:T(1024)S(1)} %fusion.22), kind=kCustom, calls=%fused_computation.5 | custom fusion | bytes 33558528 | tf_op jit(solution)/shard_map/jit(_take)/gather | solution.py:51
  2440.1 25.0 copy.68
  2465.1 54.2 %gather_fusion = f32[2048,2,1024]{2,1,0:T(2,128)} fusion(f32[4096,2,1024]{2,1,0:T(2,128)} %copy.62, s32[2048]{0:T(1024)S(1)} %fusion.19), kind=kCustom, calls=%fused_computation.4 | custom fusion | bytes 33562624 | tf_op jit(solution)/shard_map/jit(_take)/gather | solution.py:51
  2548.9 19.2 fusion.31
  2568.7 17.8 fusion.1
  2586.6 16.7 fusion.3
  2603.3 13.8 fusion.2
  2630.7 13.8 add_bitcast_fusion.1
  2647.1 51.4 %reduce-scatter.3.cloned.1.call-done = f32[256,2,512]{2,0,1:T(8,128)} async-done(((f32[1024,2,512]{2,0,1:T(8,128)}), f32[256,2,512]{2,0,1:T(8,128)}) %reduce-scatter.3.cloned.1.call-update) | async-done | bytes 1048592 | tf_op jit(solution)/shard_map/reduce_scatter | solution.py:138
  2700.9 52.7 %all-gather.5.cloned.1.call-done = f32[1024,2,512]{2,0,1:T(8,128)} async-done(((f32[256,2,512]{2,0,1:T(8,128)}), f32[1024,2,512]{2,0,1:T(8,128)}) %all-gather.5.cloned.1.call-update) | async-done | bytes 4194320 | tf_op jit(solution)/shard_map/all_gather | solution.py:142
  2753.5 17.2 fusion.6
  2770.8 16.0 fusion.7
  2786.8 15.1 add_bitcast_fusion
  2801.9 15.1 subtract_bitcast_fusion
  2821.3 89.7 %reduce-scatter.5.cloned.1.call-done = f32[256,2,512]{2,0,1:T(8,128)} async-done(((f32[2048,2,512]{2,0,1:T(8,128)}), f32[256,2,512]{2,0,1:T(8,128)}) %reduce-scatter.5.cloned.1.call-update) | async-done | bytes 1048592 | tf_op jit(solution)/shard_map/reduce_scatter | solution.py:147
  (111 shorter events, 143.5 us)
Async XLA Ops:
  22.1 12.5 all-to-all-start.4
  35.1 10.7 all-to-all-start
  45.9 49.6 %all-to-all-start.5 = ((s32[512,1,4]{0,1,2:T(1,128)}), s32[512,1,4]{0,1,2:T(1,128)S(1)}, u32[]{:S(2)}, u32[]{:S(2)}) async-start(s32[512,1,4]{0,1,2:T(1,128)} %copy.64), calls=%async_computation.5 | async-start | bytes 16384 | tf_op jit(solution)/shard_map/all_to_all | solution.py:92
  95.5 0.6 copy-start.5
  96.1 99.9 %all-to-all-start.1 = ((s32[8,4,128]{2,0,1:T(8,128)}), s32[8,4,128]{2,0,1:T(8,128)S(1)}, u32[]{:S(2)}, u32[]{:S(2)}) async-start(s32[8,4,128]{2,0,1:T(8,128)} %bitcast.137), calls=%async_computation.1 | async-start | bytes 32768 | tf_op jit(solution)/shard_map/all_to_all | solution.py:117
  196.0 0.6 copy-start.3
  196.6 730.5 %all-to-all-start.2 = ((f32[512,2,8,1024]{0,3,1,2:T(8,128)}), f32[512,2,8,1024]{0,3,1,2:T(8,128)}, u32[]{:S(2)}, u32[]{:S(2)}) async-start(f32[512,2,8,1024]{0,3,1,2:T(8,128)} %copy.58), calls=%async_computation.2 | async-start | bytes 67108864 | tf_op jit(solution)/shard_map/all_to_all | solution.py:110
  927.0 730.4 %all-to-all-start.6 = ((f32[512,2,4,2048]{3,1,2,0:T(2,128)}), f32[512,2,4,2048]{3,1,2,0:T(2,128)}, u32[]{:S(2)}, u32[]{:S(2)}) async-start(f32[512,2,4,2048]{3,1,2,0:T(2,128)} %bitcast.142), calls=%async_computation.6 | async-start | bytes 67108864 | tf_op jit(solution)/shard_map/all_to_all | solution.py:81
  1657.4 372.0 %all-to-all-start.3 = ((f32[8,4,128,2,1024]{4,2,3,0,1:T(8,128)}), f32[8,4,128,2,1024]{4,2,3,0,1:T(8,128)}, u32[]{:S(2)}, u32[]{:S(2)}) async-start(f32[8,4,128,2,1024]{4,2,3,0,1:T(8,128)} %copy.60), calls=%async_computation.3 | async-start | bytes 67108864 | tf_op jit(solution)/shard_map/all_to_all | solution.py:116
  1710.0 329.9 %copy-start.7 = (s32[8,16]{1,0:T(8,128)S(1)}, s32[8,16]{1,0:T(8,128)}, u32[]{:S(2)}) copy-start(s32[8,16]{1,0:T(8,128)} %param.14) | copy-start | bytes 1540
  1710.0 330.0 %copy-start.6 = (s32[512,1,4]{0,1,2:T(1,128)S(1)}, s32[512,1,4]{0,1,2:T(1,128)}, u32[]{:S(2)}) copy-start(s32[512,1,4]{0,1,2:T(1,128)} %copy-done.5) | copy-start | bytes 24580
  1710.0 338.1 %copy-start.4 = (s32[8,4,128]{2,0,1:T(8,128)S(1)}, s32[8,4,128]{2,0,1:T(8,128)}, u32[]{:S(2)}) copy-start(s32[8,4,128]{2,0,1:T(8,128)} %copy-done.3) | copy-start | bytes 49156
  2029.4 371.3 %all-to-all-start.7 = ((f32[4,512,2,1,2048]{4,2,1,3,0:T(2,128)}), f32[4,512,2,1,2048]{4,2,1,3,0:T(2,128)}, u32[]{:S(2)}, u32[]{:S(2)}) async-start(f32[4,512,2,1,2048]{4,2,1,3,0:T(2,128)} %pad_maximum_fusion), calls=%async_computation.7 | async-start | bytes 67108864 | tf_op jit(solution)/shard_map/all_to_all | solution.py:78
  2039.1 547.5 %all-gather.3.cloned.1.call-start = ((), (), s32[]{:S(2)}) async-start(), calls=%async_computation.10 | async-start | bytes 9437184 | tf_op jit(solution)/shard_map/all_gather | solution.py:133
  2039.8 658.6 %reduce-scatter.3.cloned.1.call-start = ((), (), s32[]{:S(2)}) async-start(), calls=%async_computation.11 | async-start | bytes 5242880 | tf_op jit(solution)/shard_map/reduce_scatter | solution.py:138
  2519.3 16.5 copy-start.1
  2586.6 16.7 copy-start
  2586.6 16.8 copy-start.10
  2603.3 27.3 slice-start.2
  2617.1 13.6 slice-start.3
  2644.5 2.5 copy-start.8
  2644.5 2.5 copy-start.9
  2646.9 106.6 %all-gather.5.cloned.1.call-start = ((), (), s32[]{:S(2)}) async-start(), calls=%async_computation.12 | async-start | bytes 5242880 | tf_op jit(solution)/shard_map/all_gather | solution.py:142
  2700.8 210.2 %reduce-scatter.5.cloned.1.call-start = ((), (), s32[]{:S(2)}) async-start(), calls=%async_computation.13 | async-start | bytes 9437184 | tf_op jit(solution)/shard_map/reduce_scatter | solution.py:147
  2753.5 17.2 copy-start.2
  2753.5 33.2 %slice-start = ((s8[8388608]{0:T(1024)(128)(4,1)}), s8[4194304]{0:T(1024)(128)(4,1)S(1)}, s32[]{:S(2)}) async-start(s8[8388608]{0:T(1024)(128)(4,1)} %bitcast.146), calls=%async_computation.14 | async-start | bytes 8388608
  2770.8 16.0 slice-start.1
Sparse Core Ops, SparseCore 0:
  2041.5 81.8 all-gather.2
  2647.0 51.3 reduce-scatter.2
  2700.9 52.5 all-gather.4
  2821.4 89.5 reduce-scatter.4
